TPU v7x, 256 devices: a whole 4x4x8 slice. The times are simulated.
256 devices in a mesh: seq: 8 (over z_hi, core), expert: 16 (over y, x), tensor: 2 (over z_lo).
Axes of the slice: x: 4, y: 4, z: 8 (z_hi: 4, z_lo: 2; z = z_hi * 2 + z_lo), core: 2. Of those that a mesh axis runs over, the one named last changes fastest.
Arguments:
- q_rows: bfloat16 [16, 1024, 4096], P('expert', 'seq', 'tensor'), may hold values from -6 to 6
- k_rows: bfloat16 [16, 1024, 512], P('expert', 'seq', 'tensor'), may hold values from -6 to 6
- value_rows: bfloat16 [16, 1024, 512], P('expert', 'seq', 'tensor'), may hold values from -6 to 6
- x_rows: bfloat16 [16, 1024, 2048], P('expert', 'seq'), may hold values from -40 to 40
- out_weight: bfloat16 [4096, 2048], P('tensor', 'expert'), may hold values from -0.09375 to 0.09375
- norm_gain: float32 [2048], P('tensor'), may hold values from 0.1 to 1.9
- w_gate: bfloat16 [128, 2048, 768], P(('seq', 'expert'), None, 'tensor'), may hold values from -0.125 to 0.125
- w_up: bfloat16 [128, 2048, 768], P(('seq', 'expert'), None, 'tensor'), may hold values from -0.125 to 0.125
- w_down: bfloat16 [128, 768, 2048], P(('seq', 'expert'), 'tensor'), may hold values from -0.21875 to 0.21875
- expert_ids: int32 [16, 1024, 8], P('expert', 'seq'), may hold values from 0 to 127, all different within a row; in each aligned block of 128 rows (0 to 127, 128 to 255, ..., all dimensions but the last counted through in order) at most 12 rows name the same one
- gate_weights: float32 [16, 1024, 8], P('expert', 'seq'), may hold values from 0.02 to 0.4
Outputs:
- layer_out: bfloat16 [16, 1024, 2048], P('expert', 'seq', 'tensor')
Inputs may be any that keep to these rules, and one draw needn't show every extreme that they name: `expert_ids`: in each token's row the 8 ids differ. Among the 128 tokens of one block of positions (the blocks laid session after session) no expert is named more than 12 times, a bound that some block reaches; every expert is named somewhere.
All inputs are finite; a program needn't handle non-finite values.
Results may differ from a plain program's by a relative error of at most 0.007.
Values may be sent and summed in bfloat16 or wider, within the bound.
A program may use at most 128 MiB of HBM per device.

v0:
```python
import math
import jax
import jax.numpy as jnp
from jax import lax
from jax.sharding import PartitionSpec as P

HEAD_SIZE = 128
TOPK = 8


def in_one_piece(arrays, axis, dim, along):
    widths = [a.shape[along] for a in arrays]
    both = jnp.concatenate(arrays, axis=along)
    out = lax.all_gather(both, axis, axis=dim, tiled=True)
    return tuple(jnp.split(out, [sum(widths[:k]) for k in range(1, len(widths))], axis=along))


def split_up(shard, dim, devices):
    before, after = (shard.shape[:dim], shard.shape[dim + 1 :])
    return jnp.moveaxis(shard.reshape(*before, devices, -1, *after), dim, 0)


def summed_on_arrival(shard, axis, dim):
    devices = lax.axis_size(axis)
    blocks = lax.all_to_all(split_up(shard, dim, devices), axis, 0, 0, tiled=True)
    return jnp.sum(blocks.astype(jnp.float32), axis=0)


def copy_for_each(shard, axis):
    copies = jnp.broadcast_to(shard, (lax.axis_size(axis), *shard.shape))
    return lax.all_to_all(copies, axis, split_axis=0, concat_axis=0, tiled=True)


def taken_together(shard, axis):
    everything = copy_for_each(shard, axis)
    return jnp.sum(everything, axis=0)


def joined_along(blocks, dim):
    blocks = jnp.moveaxis(blocks, 0, dim)
    dims = blocks.shape
    return blocks.reshape(*dims[:dim], dims[dim] * dims[dim + 1], *dims[dim + 2 :])


def one_exchange(shard, axis, axes, splits, concats):
    sizes = [lax.axis_size(a) for a in axes]
    blocks = split_up(shard, splits[0], sizes[0])
    blocks = jnp.moveaxis(split_up(blocks, splits[1] + 1, sizes[1]), 0, 1)
    inside = blocks.shape[2:]
    blocks = blocks.reshape(-1, *inside)
    blocks = lax.all_to_all(blocks, axis, split_axis=0, concat_axis=0, tiled=True)
    blocks = joined_along(blocks.reshape(*sizes, *inside), concats[0] + 1)
    return joined_along(blocks, concats[1])


def collect(shard, axis, dim):
    return joined_along(copy_for_each(shard, axis), dim)


def per_device(
    q_rows,
    k_rows,
    value_rows,
    x_rows,
    out_weight,
    norm_gain,
    w_gate,
    w_up,
    w_down,
    expert_ids,
    gate_weights,
):
    rows_here = q_rows.shape[1]
    kv_heads = k_rows.shape[2] // HEAD_SIZE
    q_heads = q_rows.shape[2] // HEAD_SIZE
    group_width = q_heads // kv_heads
    queries = q_rows[0].reshape(rows_here, kv_heads, group_width, HEAD_SIZE)
    offset = lax.axis_index("seq") * rows_here
    query_pos = offset + jnp.arange(rows_here, dtype=jnp.int32)
    softmax_scale = 1.0 / math.sqrt(HEAD_SIZE)
    tensor_pos = lax.axis_index("tensor")
    tensor_count = lax.axis_size("tensor")
    full_gate, full_up = in_one_piece((w_gate[0], w_up[0]), "tensor", 1, 0)
    full_down = lax.all_gather(w_down[0], "tensor", axis=0, tiled=True)
    pieces = in_one_piece((k_rows, value_rows), "seq", 1, 0)
    running_max = jnp.full((kv_heads, group_width, rows_here), -1e30, jnp.float32)
    block_rows = pieces[0].shape[1]
    key_block = pieces[0][0].reshape(block_rows, kv_heads, HEAD_SIZE)
    value_block = pieces[1][0].reshape(block_rows, kv_heads, HEAD_SIZE)
    scores = (
        jnp.einsum("igrd,jgd->grij", queries, key_block, preferred_element_type=jnp.float32)
        * softmax_scale
    )
    key_pos = jnp.arange(block_rows, dtype=jnp.int32)
    allowed = key_pos[None, :] <= query_pos[:, None]
    scores = jnp.where(allowed, scores, jnp.float32(-1e30))
    new_max = jnp.maximum(running_max, jnp.max(scores, axis=-1))
    weights = jnp.where(allowed, jnp.exp(scores - new_max[..., None]), jnp.float32(0.0))
    running_sum = jnp.sum(weights, axis=-1)
    weighted = jnp.einsum(
        "grij,jgd->grid",
        weights.astype(jnp.bfloat16),
        value_block,
        preferred_element_type=jnp.float32,
    )
    running_max, running_sum, weighted = (new_max, running_sum, weighted)
    attn_rows = (
        (weighted / running_sum[..., None])
        .transpose(2, 0, 1, 3)
        .reshape(rows_here, q_heads * HEAD_SIZE)
        .astype(jnp.bfloat16)
    )
    head_terms = jnp.dot(
        attn_rows,
        lax.all_gather(out_weight, "expert", axis=1, tiled=True),
        preferred_element_type=jnp.float32,
    )
    width = x_rows.shape[2]
    half_width = width // tensor_count
    share_sum = summed_on_arrival(head_terms.astype(jnp.bfloat16), "tensor", 1)
    mixed_half = (
        lax.dynamic_slice_in_dim(x_rows[0], tensor_pos * half_width, half_width, 1).astype(
            jnp.float32
        )
        + share_sum
    )
    power = taken_together(jnp.sum(mixed_half * mixed_half, axis=1), "tensor")
    inverse = lax.rsqrt(power / width + 1e-06)
    normed = (mixed_half * inverse[:, None] * norm_gain[None, :]).astype(jnp.bfloat16)
    seq_count = lax.axis_size("seq")
    group_count = lax.axis_size("expert")
    experts = seq_count * group_count
    capacity = max(2, 3 * rows_here * TOPK // (2 * experts))
    routed = expert_ids[0].reshape(-1)
    assigned = routed.shape[0]
    member = (routed[:, None] == jnp.arange(experts, dtype=jnp.int32)[None, :]).astype(jnp.int32)
    earlier = jnp.cumsum(member, axis=0) - member
    slot_index = jnp.sum(earlier * member, axis=1)
    target = routed * capacity + slot_index
    owner_index = (
        jnp.full((experts * capacity,), assigned, jnp.int32)
        .at[target]
        .set(jnp.arange(assigned, dtype=jnp.int32))
    )
    filled = owner_index < assigned
    source = jnp.minimum(owner_index // TOPK, rows_here - 1)
    whole_normed = collect(normed, "tensor", 1)
    outgoing = jnp.where(
        filled[:, None], whole_normed[source], jnp.zeros((), jnp.bfloat16)
    ).reshape(experts, capacity, width)
    half_cap = capacity // tensor_count
    my_slots = lax.dynamic_slice_in_dim(outgoing, tensor_pos * half_cap, half_cap, 1)
    hidden_half = full_down.shape[0] // tensor_count
    grouped = my_slots.reshape((seq_count, group_count) + my_slots.shape[1:])
    arrived = one_exchange(grouped, ("seq", "expert"), ("seq", "expert"), (0, 1), (0, 1))
    whole_arrived = arrived.reshape((experts,) + my_slots.shape[1:])
    flat_rows = whole_arrived.reshape(-1, width)
    gate_act = jnp.dot(flat_rows, full_gate, preferred_element_type=jnp.float32)
    up_act = jnp.dot(flat_rows, full_up, preferred_element_type=jnp.float32)
    hidden = (jax.nn.silu(gate_act) * up_act).astype(jnp.bfloat16)
    total = jnp.zeros((flat_rows.shape[0], width), jnp.float32)
    for group_pos in range(tensor_count):
        lo_col = group_pos * hidden_half
        piece = jnp.dot(
            hidden[:, lo_col : lo_col + hidden_half],
            full_down[lo_col : lo_col + hidden_half],
            preferred_element_type=jnp.float32,
        )
        total = total + piece.astype(jnp.bfloat16).astype(jnp.float32)
    finished = total.astype(jnp.bfloat16).reshape(whole_arrived.shape)
    finished = finished.reshape((seq_count, group_count) + finished.shape[1:])
    returned = one_exchange(finished, ("seq", "expert"), ("seq", "expert"), (0, 1), (0, 1))
    back_whole = returned.reshape((experts,) + returned.shape[2:])
    returned = lax.all_to_all(back_whole, "tensor", split_axis=2, concat_axis=1, tiled=True)
    came_back = returned.reshape(experts * capacity, half_width)
    picked = came_back[target].astype(jnp.float32)
    weights_flat = gate_weights[0].reshape(-1)
    blended = jnp.sum((picked * weights_flat[:, None]).reshape(rows_here, TOPK, half_width), axis=1)
    return (mixed_half + blended).astype(jnp.bfloat16)[None]


def solution(mesh):
    return jax.shard_map(
        per_device,
        mesh=mesh,
        in_specs=(
            P("expert", "seq", "tensor"),
            P("expert", "seq", "tensor"),
            P("expert", "seq", "tensor"),
            P("expert", "seq", None),
            P("tensor", "expert"),
            P("tensor"),
            P(("seq", "expert"), None, "tensor"),
            P(("seq", "expert"), None, "tensor"),
            P(("seq", "expert"), "tensor", None),
            P("expert", "seq", None),
            P("expert", "seq", None),
        ),
        out_specs=P("expert", "seq", "tensor"),
        check_vma=False,
    )
```

profile of v0, /device:TPU:1, one launch (start us, length us, event | category | flops | bytes accessed | tf_op | source)
XLA Modules:
  0.0 554.6 jit_solution(8807647525143231353)
XLA Ops:
  6.5 0.9 copy.93
  7.5 1.0 copy.94
  8.5 0.7 pad_maximum_fusion.1
  9.1 0.0 all-gather.6.cloned.1.call-update
  9.2 0.0 all-gather.8.cloned.1.call-start
  9.2 0.7 all-gather.8.cloned.1.call-update
  9.9 0.0 all-gather.10.cloned.1.call-start
  10.0 3.9 pad_maximum_fusion
  13.9 0.1 copy.100
  14.0 0.1 eq.29
  14.1 0.1 eq.25
  14.2 0.1 iota_compare_fusion.2
  14.3 0.1 copy.119
  14.5 0.1 copy.102
  14.6 0.2 fusion.28
  14.8 30.4 %all-gather.6.cloned.1.call-done = bf16[2,1024,256]{1,2,0:T(8,128)(2,1)} async-done(((bf16[2,128,256]{1,2,0:T(8,128)(2,1)}), bf16[2,1024,256]{1,2,0:T(8,128)(2,1)}) %all-gather.6.cloned.1.call-update) | async-done | bytes 1048592 | tf_op jit(solution)/shard_map/all_gather | solution.py:14
  45.2 1.3 fusion.39
  46.5 1.5 fusion
  48.0 2.0 fusion.1
  50.0 2.1 divide_convert_fusion
  52.1 76.2 %all-gather.8.cloned.1.call-done = bf16[2048,2048]{1,0:T(8,128)(2,1)} async-done(((bf16[2048,128]{1,0:T(8,128)(2,1)}), bf16[2048,2048]{1,0:T(8,128)(2,1)}) %all-gather.8.cloned.1.call-update) | async-done | bytes 8388624 | tf_op jit(solution)/shard_map/all_gather | solution.py:115
  128.3 4.7 convolution_convert_fusion.2
  133.0 0.8 copy.125
  133.8 3.5 all-to-all-start
  137.4 0.1 copy.103
  137.5 0.1 copy.99
  137.6 0.1 mul.81
  137.7 0.4 fusion.25
  138.1 5.7 %all-to-all-done = bf16[2,128,1024]{2,1,0:T(8,128)(2,1)S(1)} async-done(((bf16[2,128,1024]{2,1,0:T(8,128)(2,1)}), bf16[2,128,1024]{2,1,0:T(8,128)(2,1)S(1)}, u32[]{:S(2)}, u32[]{:S(2)}) %all-to-all-start) | async-done | bytes 524320 | tf_op jit(solution)/shard_map/all_to_all | solution.py:25
  143.8 0.1 convert_reduce_fusion
  143.9 0.2 multiply_reduce_fusion
  144.0 0.6 broadcast_in_dim.55
  144.6 3.2 all-to-all-start.1
  147.9 4.3 scatter_custom_fusion
  152.2 0.1 multiply_convert_fusion.1
  152.4 0.9 broadcast_in_dim.56
  153.2 3.7 all-to-all-start.2
  156.9 0.1 broadcast_in_dim.53
  157.1 0.1 constant_dynamic-slice_fusion
  157.2 12.9 %all-to-all-done.2 = bf16[2,128,1024]{2,1,0:T(8,128)(2,1)S(1)} async-done(((bf16[2,128,1024]{2,1,0:T(8,128)(2,1)}), bf16[2,128,1024]{2,1,0:T(8,128)(2,1)S(1)}, u32[]{:S(2)}, u32[]{:S(2)}) %all-to-all-start.2) | async-done | bytes 524320 | tf_op jit(solution)/shard_map/all_to_all | solution.py:31
  170.2 7.1 %gather_fusion = bf16[1536,2048]{1,0:T(8,128)(2,1)} fusion(bf16[128,2048]{1,0:T(8,128)(2,1)S(1)} %bitcast.108, s32[2048]{0:T(1024)S(1)} %pad_clamp_fusion), kind=kCustom, calls=%fused_computation | custom fusion | bytes 12589056 | tf_op jit(solution)/shard_map/gather | solution.py:149
  177.2 10.6 %gather.9 = bf16[128,12,2048]{2,1,0:T(8,128)(2,1)} reshape(bf16[1536,2048]{1,0:T(8,128)(2,1)} %gather_fusion) | data formatting | bytes 12582912 | tf_op jit(solution)/shard_map/gather | solution.py:149
  187.8 6.0 %fusion.3 = bf16[128,1,1,6,2048]{4,3,2,1,0:T(8,128)(2,1)} fusion(bf16[128,12,2048]{2,1,0:T(8,128)(2,1)} %gather.9, s32[]{:T(128)S(6)} %select_n.44, pred[128,6]{1,0:T(8,128)(4,1)S(1)} %constant_dynamic-slice_fusion), kind=kLoop, calls=%fused_computation.10 | loop fusion | flops 1572864 | bytes 6292228 | tf_op jit(solution)/shard_map/reshape;transpose;transpose;reshape;reshape;reshape | solution.py:50
  193.8 15.1 %all-to-all-start.3 = ((bf16[128,1,1,6,2048]{4,3,2,1,0:T(8,128)(2,1)}), bf16[128,1,1,6,2048]{4,3,2,1,0:T(8,128)(2,1)}, u32[]{:S(2)}, u32[]{:S(2)}) async-start(bf16[128,1,1,6,2048]{4,3,2,1,0:T(8,128)(2,1)} %fusion.3), calls=%async_computation.3 | async-start | bytes 8388608 | tf_op jit(solution)/shard_map/all_to_all | solution.py:51
  208.9 0.0 all-gather.12.cloned.1.call-start
  208.9 0.5 all-gather.12.cloned.1.call-update
  209.4 127.5 %all-to-all-done.3 = bf16[128,1,1,6,2048]{4,3,2,1,0:T(8,128)(2,1)} async-done(((bf16[128,1,1,6,2048]{4,3,2,1,0:T(8,128)(2,1)}), bf16[128,1,1,6,2048]{4,3,2,1,0:T(8,128)(2,1)}, u32[]{:S(2)}, u32[]{:S(2)}) %all-to-all-start.3) | async-done | bytes 3145760 | tf_op jit(solution)/shard_map/all_to_all | solution.py:51
  336.9 4.9 reshape_reshape_reshape.3
  341.8 0.0 all-gather.10.cloned.1.call-done
  341.8 4.6 fusion.10
  346.5 3.8 multiply_convert_fusion
  350.3 3.5 convolution_convert_fusion
  353.8 1.8 add_convert_fusion
  355.6 2.9 reshape_transpose_transpose_reshape_reshape_reshape_reshape.3
  358.5 107.2 %all_to_all.41 = bf16[128,1,1,6,2048]{4,3,2,1,0:T(8,128)(2,1)} all-to-all(bf16[128,1,1,6,2048]{4,3,2,1,0:T(8,128)(2,1)} %bitcast.109), channel_id=1, replica_groups=mesh['seq'=8,'expert'=16,'tensor'=2] {'seq','expert'}, dimensions={0} | all-to-all | bytes 6291456 | tf_op jit(solution)/shard_map/all_to_all | solution.py:51
  465.7 7.2 %copy.108 = bf16[128,6,2048]{0,1,2:T(8,128)(2,1)} copy(bf16[128,6,2048]{2,1,0:T(8,128)(2,1)} %bitcast.111) | data formatting | bytes 6291456 | tf_op jit(solution)/shard_map/reshape;reshape | solution.py:173
  472.9 6.0 %all-to-all-start.5 = ((bf16[128,6,2048]{0,1,2:T(8,128)(2,1)}), bf16[128,6,2048]{0,1,2:T(8,128)(2,1)}, u32[]{:S(2)}, u32[]{:S(2)}) async-start(bf16[128,6,2048]{0,1,2:T(8,128)(2,1)} %copy.108), calls=%async_computation.5 | async-start | bytes 8388608 | tf_op jit(solution)/shard_map/all_to_all | solution.py:174
  478.9 0.1 copy.110
  479.0 46.5 %all-to-all-done.5 = bf16[128,6,2048]{0,1,2:T(8,128)(2,1)} async-done(((bf16[128,6,2048]{0,1,2:T(8,128)(2,1)}), bf16[128,6,2048]{0,1,2:T(8,128)(2,1)}, u32[]{:S(2)}, u32[]{:S(2)}) %all-to-all-start.5) | async-done | bytes 3145760 | tf_op jit(solution)/shard_map/all_to_all | solution.py:174
  525.5 7.4 %copy.109 = bf16[128,6,2,1024]{3,1,2,0:T(8,128)(2,1)} copy(bf16[128,6,2,1024]{0,1,3,2:T(8,128)(2,1)} %bitcast.35) | data formatting | bytes 6291456 | tf_op jit(solution)/shard_map/all_to_all | solution.py:174
  533.0 4.9 reshape.117
  537.8 5.3 gather_fusion.1
  543.2 2.9 fusion.4
  546.1 1.9 fusion.22
  (41 shorter events, 0.3 us)
Async XLA Ops:
  6.5 38.7 %all-gather.6.cloned.1.call-start = ((), (), s32[]{:S(2)}) async-start(), calls=%async_computation.6 | async-start | bytes 1179648 | tf_op jit(solution)/shard_map/all_gather | solution.py:14
  9.2 119.1 %all-gather.8.cloned.1.call-start = ((), (), s32[]{:S(2)}) async-start(), calls=%async_computation.7 | async-start | bytes 8912896 | tf_op jit(solution)/shard_map/all_gather | solution.py:115
  9.9 331.9 %all-gather.10.cloned.1.call-start = ((), (), s32[]{:S(2)}) async-start(), calls=%async_computation.8 | async-start | bytes 9437184 | tf_op jit(solution)/shard_map/all_gather | solution.py:14
  10.0 4.0 copy-start.4
  10.0 4.4 copy-start.2
  14.8 33.1 %copy-start.3 = (s32[128,9]{0,1:T(8,128)}, s32[128,9]{0,1:T(8,128)S(1)}, u32[]{:S(2)}) copy-start(s32[128,9]{0,1:T(8,128)S(1)} %reduce-window.9) | copy-start | bytes 13828
  128.3 9.0 %slice-start = ((s32[128,9]{0,1:T(8,128)}), s32[128,8]{0,1:T(8,128)S(1)}, s32[]{:S(2)}) async-start(s32[128,9]{0,1:T(8,128)} %copy-done.3), calls=%async_computation.10 | async-start | bytes 8192 | tf_op jit(solution)/shard_map/slice.1
  133.0 10.9 %copy-start.1 = (bf16[1,128,2048]{2,1,0:T(8,128)(2,1)S(1)}, bf16[1,128,2048]{2,1,0:T(8,128)(2,1)}, u32[]{:S(2)}) copy-start(bf16[1,128,2048]{2,1,0:T(8,128)(2,1)} %param.14) | copy-start | bytes 1572868
  133.0 19.2 %copy-start.5 = (f32[1024]{0:T(1024)S(1)}, f32[1024]{0:T(1024)}, u32[]{:S(2)}) copy-start(f32[1024]{0:T(1024)} %param.16) | copy-start | bytes 12292
  133.8 9.9 %all-to-all-start = ((bf16[2,128,1024]{2,1,0:T(8,128)(2,1)}), bf16[2,128,1024]{2,1,0:T(8,128)(2,1)S(1)}, u32[]{:S(2)}, u32[]{:S(2)}) async-start(bf16[2,128,1024]{2,1,0:T(8,128)(2,1)} %bitcast.107), calls=%async_computation | async-start | bytes 1048576 | tf_op jit(solution)/shard_map/all_to_all | solution.py:25
  143.9 26.2 %copy-start = (f32[128,1024]{1,0:T(8,128)}, f32[128,1024]{1,0:T(8,128)S(1)}, u32[]{:S(2)}) copy-start(f32[128,1024]{1,0:T(8,128)S(1)} %convert_reduce_fusion) | copy-start | bytes 1572868
  144.6 7.6 %all-to-all-start.1 = ((f32[2,1,128]{2,1,0:T(1,128)}), f32[2,1,128]{2,1,0:T(1,128)S(1)}, u32[]{:S(2)}, u32[]{:S(2)}) async-start(f32[2,1,128]{2,1,0:T(1,128)} %broadcast_in_dim.55), calls=%async_computation.1 | async-start | bytes 2048 | tf_op jit(solution)/shard_map/all_to_all | solution.py:31
  153.2 16.9 %all-to-all-start.2 = ((bf16[2,128,1024]{2,1,0:T(8,128)(2,1)}), bf16[2,128,1024]{2,1,0:T(8,128)(2,1)S(1)}, u32[]{:S(2)}, u32[]{:S(2)}) async-start(bf16[2,128,1024]{2,1,0:T(8,128)(2,1)} %broadcast_in_dim.56), calls=%async_computation.2 | async-start | bytes 1048576 | tf_op jit(solution)/shard_map/all_to_all | solution.py:31
  193.8 143.1 %all-to-all-start.3 = ((bf16[128,1,1,6,2048]{4,3,2,1,0:T(8,128)(2,1)}), bf16[128,1,1,6,2048]{4,3,2,1,0:T(8,128)(2,1)}, u32[]{:S(2)}, u32[]{:S(2)}) async-start(bf16[128,1,1,6,2048]{4,3,2,1,0:T(8,128)(2,1)} %fusion.3), calls=%async_computation.3 | async-start | bytes 8388608 | tf_op jit(solution)/shard_map/all_to_all | solution.py:51
  208.9 141.4 %all-gather.12.cloned.1.call-start = ((), (), s32[]{:S(2)}) async-start(), calls=%async_computation.9 | async-start | bytes 4718592 | tf_op jit(solution)/shard_map/all_gather | solution.py:84
  341.8 4.7 copy-start.7
  350.3 3.5 copy-start.8
  350.3 3.5 copy-start.9
  472.9 6.0 %copy-start.6 = (f32[1,128,8]{1,2,0:T(8,128)S(1)}, f32[1,128,8]{1,2,0:T(8,128)}, u32[]{:S(2)}) copy-start(f32[1,128,8]{1,2,0:T(8,128)} %param.21) | copy-start | bytes 12292
  472.9 52.6 %all-to-all-start.5 = ((bf16[128,6,2048]{0,1,2:T(8,128)(2,1)}), bf16[128,6,2048]{0,1,2:T(8,128)(2,1)}, u32[]{:S(2)}, u32[]{:S(2)}) async-start(bf16[128,6,2048]{0,1,2:T(8,128)(2,1)} %copy.108), calls=%async_computation.5 | async-start | bytes 8388608 | tf_op jit(solution)/shard_map/all_to_all | solution.py:174
Sparse Core Ops, SparseCore 0:
  9.3 35.8 all-gather.5
  47.6 80.6 all-gather.7
  130.1 131.7 all-gather.9
  263.6 81.7 all-gather.11
where the time goes:
time: 556 us; the launch traced here: 555 us
  waiting for transfers between devices  300 us (54%)
  blocking collectives  107 us (19%)
  local copies, waits for them, and re-layouts  61.2 us (11%)
  starting transfers between devices  31.5 us (6%)
  matrix products  22 us (4%)
  other arithmetic  18.6 us (3%)
  between operations  13.6 us (2%)
    all_to_all x1, waiting for transfers between devices, one_exchange(): lax.all_to_all(blocks, axis, split_axis=0, concat_axis=0, tiled=True)  127 us
    all_to_all x1, blocking collectives, one_exchange(): lax.all_to_all(blocks, axis, split_axis=0, concat_axis=0, tiled=True)  107 us
    all_gather x1, waiting for transfers between devices, per_device(): lax.all_gather(out_weight, 'expert', axis=1, tiled=True)  76.2 us
    all_to_all x1, waiting for transfers between devices, per_device(): lax.all_to_all(back_whole, 'tensor', split_axis=2, concat_axis=1, tiled=T...  46.5 us
    all_gather x2, waiting for transfers between devices, in_one_piece(): out = lax.all_gather(both, axis, axis=dim, tiled=True)  30.4 us
    gather x2, local copies, waits for them, and re-layouts, per_device(): whole_normed[source]  17.7 us
    all_to_all x1, starting transfers between devices, one_exchange(): lax.all_to_all(blocks, axis, split_axis=0, concat_axis=0, tiled=True)  15.1 us
    all_to_all x2, waiting for transfers between devices, copy_for_each(): return lax.all_to_all(copies, axis, split_axis=0, concat_axis=0, tiled=True)  13 us
  transfers between devices with their start and end apart: 9, of which 6 were waited for; matrix products, arithmetic and copies ran while one was open for 11% of the time, Pallas kernels for 0%

commit v1 on v0

--- a/solution.py
+++ b/solution.py
@@ -3,6 +3,7 @@
 import jax.numpy as jnp
 from jax import lax
 from jax.sharding import PartitionSpec as P
+from jax.lax import all_to_all, psum
 
 HEAD_SIZE = 128
 TOPK = 8
@@ -171,7 +172,14 @@
     finished = finished.reshape((seq_count, group_count) + finished.shape[1:])
     returned = one_exchange(finished, ("seq", "expert"), ("seq", "expert"), (0, 1), (0, 1))
     back_whole = returned.reshape((experts,) + returned.shape[2:])
-    returned = lax.all_to_all(back_whole, "tensor", split_axis=2, concat_axis=1, tiled=True)
+
+    def meet_plane_up(u):
+        return jnp.concatenate(
+            all_to_all(jnp.stack(jnp.split(u, psum(1, "tensor"), axis=2), 0), "tensor", 0, 0),
+            axis=1,
+        )
+
+    returned = meet_plane_up(back_whole)
     came_back = returned.reshape(experts * capacity, half_width)
     picked = came_back[target].astype(jnp.float32)
     weights_flat = gate_weights[0].reshape(-1)

time: 556 us -> 536 us (0.964)
  waiting for transfers between devices: 300 us -> 289 us
  local copies, waits for them, and re-layouts: 61.2 us -> 53.1 us
    all_to_all x1, waiting for transfers between devices: 46.5 us -> 35.3 us  [meet_plane_up(): all_to_all(jnp.stack(jnp.split(u, psum(1, 'tensor'), axis=2), 0), 'tensor...]
    all_to_all x1 -> x0, local copies, waits for them, and re-layouts: 7.42 us -> none  [per_device(): lax.all_to_all(back_whole, 'tensor', split_axis=2, concat_axis=1, tiled=T...]
where the time goes in v1:
time: 536 us; the launch traced here: 535 us
  waiting for transfers between devices  289 us (54%)
  blocking collectives  107 us (20%)
  local copies, waits for them, and re-layouts  53.1 us (10%)
  starting transfers between devices  29.8 us (6%)
  matrix products  22 us (4%)
  other arithmetic  20.4 us (4%)
  between operations  13.6 us (3%)
    all_to_all x1, waiting for transfers between devices, one_exchange(): lax.all_to_all(blocks, axis, split_axis=0, concat_axis=0, tiled=True)  127 us
    all_to_all x1, blocking collectives, one_exchange(): lax.all_to_all(blocks, axis, split_axis=0, concat_axis=0, tiled=True)  107 us
    all_gather x1, waiting for transfers between devices, per_device(): lax.all_gather(out_weight, 'expert', axis=1, tiled=True)  76.2 us
    all_to_all x1, waiting for transfers between devices, meet_plane_up(): all_to_all(jnp.stack(jnp.split(u, psum(1, 'tensor'), axis=2), 0), 'tensor...  35.3 us
    all_gather x2, waiting for transfers between devices, in_one_piece(): out = lax.all_gather(both, axis, axis=dim, tiled=True)  29.8 us
    gather x2, local copies, waits for them, and re-layouts, per_device(): whole_normed[source]  17.7 us
    all_to_all x1, starting transfers between devices, one_exchange(): lax.all_to_all(blocks, axis, split_axis=0, concat_axis=0, tiled=True)  15.1 us
    all_to_all x2, waiting for transfers between devices, copy_for_each(): return lax.all_to_all(copies, axis, split_axis=0, concat_axis=0, tiled=True)  13 us
  transfers between devices with their start and end apart: 9, of which 6 were waited for; matrix products, arithmetic and copies ran while one was open for 11% of the time, Pallas kernels for 0%

profile of v1, /device:TPU:1, one launch (start us, length us, event | category | flops | bytes accessed | tf_op | source)
XLA Modules:
  0.0 534.7 jit_solution(11986623177749765639)
XLA Ops:
  6.5 0.9 copy.61
  7.5 1.0 copy.62
  8.5 0.7 pad_maximum_fusion.2
  9.2 0.0 all-gather.8.cloned.1.call-start
  9.2 0.7 all-gather.8.cloned.1.call-update
  10.0 3.9 pad_maximum_fusion
  13.8 0.7 copy-done.4
  14.5 0.1 copy.68
  14.6 0.1 eq.29
  14.7 0.1 eq.25
  14.8 0.1 iota_compare_fusion.2
  14.9 0.1 copy.85
  15.0 0.1 copy.70
  15.1 0.2 fusion.28
  15.4 29.8 %all-gather.6.cloned.1.call-done = bf16[2,1024,256]{1,2,0:T(8,128)(2,1)} async-done(((bf16[2,128,256]{1,2,0:T(8,128)(2,1)}), bf16[2,1024,256]{1,2,0:T(8,128)(2,1)}) %all-gather.6.cloned.1.call-update) | async-done | bytes 1048592 | tf_op jit(solution)/shard_map/all_gather | solution.py:15
  45.2 1.3 fusion.39
  46.5 1.5 fusion
  48.0 2.0 fusion.1
  50.0 2.1 divide_convert_fusion
  52.1 76.2 %all-gather.8.cloned.1.call-done = bf16[2048,2048]{1,0:T(8,128)(2,1)} async-done(((bf16[2048,128]{1,0:T(8,128)(2,1)}), bf16[2048,2048]{1,0:T(8,128)(2,1)}) %all-gather.8.cloned.1.call-update) | async-done | bytes 8388624 | tf_op jit(solution)/shard_map/all_gather | solution.py:116
  128.3 4.7 convolution_convert_fusion.2
  133.0 0.8 copy.91
  133.8 3.5 all-to-all-start
  137.4 0.1 copy.71
  137.5 0.1 copy.67
  137.6 0.1 mul.81
  137.7 0.4 fusion.25
  138.1 5.7 %all-to-all-done = bf16[2,128,1024]{2,1,0:T(8,128)(2,1)S(1)} async-done(((bf16[2,128,1024]{2,1,0:T(8,128)(2,1)}), bf16[2,128,1024]{2,1,0:T(8,128)(2,1)S(1)}, u32[]{:S(2)}, u32[]{:S(2)}) %all-to-all-start) | async-done | bytes 524320 | tf_op jit(solution)/shard_map/all_to_all | solution.py:26
  143.8 0.1 convert_reduce_fusion
  143.9 0.2 multiply_reduce_fusion
  144.0 0.6 broadcast_in_dim.55
  144.6 3.2 all-to-all-start.1
  147.9 4.3 scatter_custom_fusion
  152.2 0.1 multiply_convert_fusion.1
  152.4 0.9 broadcast_in_dim.56
  153.2 3.7 all-to-all-start.2
  156.9 0.1 broadcast_in_dim.53
  157.1 0.1 constant_dynamic-slice_fusion
  157.2 12.9 %all-to-all-done.2 = bf16[2,128,1024]{2,1,0:T(8,128)(2,1)S(1)} async-done(((bf16[2,128,1024]{2,1,0:T(8,128)(2,1)}), bf16[2,128,1024]{2,1,0:T(8,128)(2,1)S(1)}, u32[]{:S(2)}, u32[]{:S(2)}) %all-to-all-start.2) | async-done | bytes 524320 | tf_op jit(solution)/shard_map/all_to_all | solution.py:32
  170.2 7.1 %gather_fusion = bf16[1536,2048]{1,0:T(8,128)(2,1)} fusion(bf16[128,2048]{1,0:T(8,128)(2,1)S(1)} %bitcast.113, s32[2048]{0:T(1024)S(1)} %pad_clamp_fusion), kind=kCustom, calls=%fused_computation | custom fusion | bytes 12589056 | tf_op jit(solution)/shard_map/gather | solution.py:150
  177.2 10.6 %gather.9 = bf16[128,12,2048]{2,1,0:T(8,128)(2,1)} reshape(bf16[1536,2048]{1,0:T(8,128)(2,1)} %gather_fusion) | data formatting | bytes 12582912 | tf_op jit(solution)/shard_map/gather | solution.py:150
  187.9 6.0 %fusion.3 = bf16[128,1,1,6,2048]{4,3,2,1,0:T(8,128)(2,1)} fusion(bf16[128,12,2048]{2,1,0:T(8,128)(2,1)} %gather.9, s32[]{:T(128)S(6)} %select_n.44, pred[128,6]{1,0:T(8,128)(4,1)S(1)} %constant_dynamic-slice_fusion), kind=kLoop, calls=%fused_computation.10 | loop fusion | flops 1572864 | bytes 6292228 | tf_op jit(solution)/shard_map/reshape;transpose;transpose;reshape;reshape;reshape | solution.py:51
  193.8 15.1 %all-to-all-start.3 = ((bf16[128,1,1,6,2048]{4,3,2,1,0:T(8,128)(2,1)}), bf16[128,1,1,6,2048]{4,3,2,1,0:T(8,128)(2,1)}, u32[]{:S(2)}, u32[]{:S(2)}) async-start(bf16[128,1,1,6,2048]{4,3,2,1,0:T(8,128)(2,1)} %fusion.3), calls=%async_computation.3 | async-start | bytes 8388608 | tf_op jit(solution)/shard_map/all_to_all | solution.py:52
  208.9 0.0 all-gather.12.cloned.1.call-start
  208.9 0.5 all-gather.12.cloned.1.call-update
  209.5 127.5 %all-to-all-done.3 = bf16[128,1,1,6,2048]{4,3,2,1,0:T(8,128)(2,1)} async-done(((bf16[128,1,1,6,2048]{4,3,2,1,0:T(8,128)(2,1)}), bf16[128,1,1,6,2048]{4,3,2,1,0:T(8,128)(2,1)}, u32[]{:S(2)}, u32[]{:S(2)}) %all-to-all-start.3) | async-done | bytes 3145760 | tf_op jit(solution)/shard_map/all_to_all | solution.py:52
  336.9 4.9 reshape_reshape_reshape.3
  341.9 4.6 fusion.10
  346.5 3.8 multiply_convert_fusion
  350.3 3.5 convolution_convert_fusion
  353.9 1.8 add_convert_fusion
  355.7 2.9 reshape_transpose_transpose_reshape_reshape_reshape_reshape.3
  358.5 107.1 %all_to_all.31 = bf16[128,1,1,6,2048]{4,3,2,1,0:T(8,128)(2,1)S(1)} all-to-all(bf16[128,1,1,6,2048]{4,3,2,1,0:T(8,128)(2,1)} %bitcast.114), channel_id=1, replica_groups=mesh['seq'=8,'expert'=16,'tensor'=2] {'seq','expert'}, dimensions={0} | all-to-all | bytes 6291456 | tf_op jit(solution)/shard_map/all_to_all | solution.py:52
  465.6 1.7 copy.75
  467.4 0.3 slice_bitcast_fusion.1
  467.7 1.9 pad_maximum_fusion.1
  469.6 4.3 all-to-all-start.5
  474.0 0.1 copy.77
  474.1 35.3 %all-to-all-done.5 = bf16[2,128,6,1024]{3,1,2,0:T(8,128)(2,1)S(1)} async-done(((bf16[2,128,6,1024]{3,1,2,0:T(8,128)(2,1)}), bf16[2,128,6,1024]{3,1,2,0:T(8,128)(2,1)S(1)}, u32[]{:S(2)}, u32[]{:S(2)}) %all-to-all-start.5) | async-done | bytes 3145760 | tf_op jit(solution)/shard_map/all_to_all | solution.py:178
  509.3 3.7 copy.76
  513.1 4.9 reshape_reshape.7
  518.0 5.4 %gather_fusion.1 = bf16[1024,1024]{1,0:T(8,128)(2,1)} fusion(bf16[1536,1024]{1,0:T(8,128)(2,1)S(1)} %reshape_reshape.7, s32[1024]{0:T(1024)S(1)} %broadcast_clamp_fusion), kind=kCustom, calls=%fused_computation.1 | custom fusion | bytes 4198400 | tf_op jit(solution)/shard_map/gather | solution.py:184
  523.3 2.9 fusion.4
  526.3 1.9 fusion.22
  (43 shorter events, 0.3 us)
Async XLA Ops:
  6.5 38.7 %all-gather.6.cloned.1.call-start = ((), (), s32[]{:S(2)}) async-start(), calls=%async_computation.6 | async-start | bytes 1179648 | tf_op jit(solution)/shard_map/all_gather | solution.py:15
  9.2 119.1 %all-gather.8.cloned.1.call-start = ((), (), s32[]{:S(2)}) async-start(), calls=%async_computation.7 | async-start | bytes 8912896 | tf_op jit(solution)/shard_map/all_gather | solution.py:116
  9.9 331.9 %all-gather.10.cloned.1.call-start = ((), (), s32[]{:S(2)}) async-start(), calls=%async_computation.8 | async-start | bytes 9437184 | tf_op jit(solution)/shard_map/all_gather | solution.py:15
  13.8 0.7 copy-start.4
  13.8 1.1 copy-start.2
  15.4 32.6 %copy-start.3 = (s32[128,9]{0,1:T(8,128)}, s32[128,9]{0,1:T(8,128)S(1)}, u32[]{:S(2)}) copy-start(s32[128,9]{0,1:T(8,128)S(1)} %reduce-window.9) | copy-start | bytes 13828
  128.3 9.0 %slice-start = ((s32[128,9]{0,1:T(8,128)}), s32[128,8]{0,1:T(8,128)S(1)}, s32[]{:S(2)}) async-start(s32[128,9]{0,1:T(8,128)} %copy-done.3), calls=%async_computation.10 | async-start | bytes 8192 | tf_op jit(solution)/shard_map/slice.1
  133.0 10.9 %copy-start.1 = (bf16[1,128,2048]{2,1,0:T(8,128)(2,1)S(1)}, bf16[1,128,2048]{2,1,0:T(8,128)(2,1)}, u32[]{:S(2)}) copy-start(bf16[1,128,2048]{2,1,0:T(8,128)(2,1)} %param.14) | copy-start | bytes 1572868
  133.0 19.3 %copy-start.5 = (f32[1024]{0:T(1024)S(1)}, f32[1024]{0:T(1024)}, u32[]{:S(2)}) copy-start(f32[1024]{0:T(1024)} %param.16) | copy-start | bytes 12292
  133.8 9.9 %all-to-all-start = ((bf16[2,128,1024]{2,1,0:T(8,128)(2,1)}), bf16[2,128,1024]{2,1,0:T(8,128)(2,1)S(1)}, u32[]{:S(2)}, u32[]{:S(2)}) async-start(bf16[2,128,1024]{2,1,0:T(8,128)(2,1)} %bitcast.112), calls=%async_computation | async-start | bytes 1048576 | tf_op jit(solution)/shard_map/all_to_all | solution.py:26
  143.9 26.3 %copy-start = (f32[128,1024]{1,0:T(8,128)}, f32[128,1024]{1,0:T(8,128)S(1)}, u32[]{:S(2)}) copy-start(f32[128,1024]{1,0:T(8,128)S(1)} %convert_reduce_fusion) | copy-start | bytes 1572868
  144.6 7.6 %all-to-all-start.1 = ((f32[2,1,128]{2,1,0:T(1,128)}), f32[2,1,128]{2,1,0:T(1,128)S(1)}, u32[]{:S(2)}, u32[]{:S(2)}) async-start(f32[2,1,128]{2,1,0:T(1,128)} %broadcast_in_dim.55), calls=%async_computation.1 | async-start | bytes 2048 | tf_op jit(solution)/shard_map/all_to_all | solution.py:32
  153.2 16.9 %all-to-all-start.2 = ((bf16[2,128,1024]{2,1,0:T(8,128)(2,1)}), bf16[2,128,1024]{2,1,0:T(8,128)(2,1)S(1)}, u32[]{:S(2)}, u32[]{:S(2)}) async-start(bf16[2,128,1024]{2,1,0:T(8,128)(2,1)} %broadcast_in_dim.56), calls=%async_computation.2 | async-start | bytes 1048576 | tf_op jit(solution)/shard_map/all_to_all | solution.py:32
  193.8 143.1 %all-to-all-start.3 = ((bf16[128,1,1,6,2048]{4,3,2,1,0:T(8,128)(2,1)}), bf16[128,1,1,6,2048]{4,3,2,1,0:T(8,128)(2,1)}, u32[]{:S(2)}, u32[]{:S(2)}) async-start(bf16[128,1,1,6,2048]{4,3,2,1,0:T(8,128)(2,1)} %fusion.3), calls=%async_computation.3 | async-start | bytes 8388608 | tf_op jit(solution)/shard_map/all_to_all | solution.py:52
  208.9 141.4 %all-gather.12.cloned.1.call-start = ((), (), s32[]{:S(2)}) async-start(), calls=%async_computation.9 | async-start | bytes 4718592 | tf_op jit(solution)/shard_map/all_gather | solution.py:85
  341.8 4.7 copy-start.7
  350.3 3.5 copy-start.8
  350.3 3.5 copy-start.9
  469.6 4.3 copy-start.6
  469.6 39.7 %all-to-all-start.5 = ((bf16[2,128,6,1024]{3,1,2,0:T(8,128)(2,1)}), bf16[2,128,6,1024]{3,1,2,0:T(8,128)(2,1)S(1)}, u32[]{:S(2)}, u32[]{:S(2)}) async-start(bf16[2,128,6,1024]{3,1,2,0:T(8,128)(2,1)} %pad_maximum_fusion.1), calls=%async_computation.5 | async-start | bytes 6291456 | tf_op jit(solution)/shard_map/all_to_all | solution.py:178
Sparse Core Ops, SparseCore 0:
  9.3 35.8 all-gather.5
  47.6 80.6 all-gather.7
  130.1 131.7 all-gather.9
  263.5 81.8 all-gather.11
